TPU v7x, 32 devices: a whole 2x2x4 slice. The times are simulated.
32 devices in a mesh: space: 4 (over y, x), orb: 8 (over z, core).
Axes of the slice: x: 2, y: 2, z: 4, core: 2. Of those that a mesh axis runs over, the one named last changes fastest.
Arguments:
- orbitals: float32 [16, 16, 32, 1024], P('space', None, None, 'orb'), may hold values from -6 to 6
- potential: float32 [16, 16, 32], P('space'), may hold values from 0 to 2
Outputs:
- updated: float32 [16, 16, 32, 1024], P('space', None, None, 'orb')
All inputs are finite; a program needn't handle non-finite values.
Results may differ from a plain program's by a relative error of at most 0.00007.
Values sent between devices are 32-bit elements; how exact they have to be, the bound alone decides.
A program may use at most 64 MiB of HBM per device.

v0:
```python
import jax
import jax.numpy as jnp
from jax import lax
from jax.sharding import PartitionSpec as P

PANEL = 512
DEGREE = 4
STENCIL = (-205.0 / 72.0, 8.0 / 5.0, -1.0 / 5.0, 8.0 / 315.0, -1.0 / 560.0)
SHIFT_MID = 7.25
HALF_WIDTH = 4.75


def padded_2(shard, sides, width):
    for axis, dim in sides:
        count, length = (lax.axis_size(axis), shard.shape[dim])
        up = [(i, (i + 1) % count) for i in range(count)]
        down = [(j, i) for i, j in up]
        last = lax.slice_in_dim(shard, length - width, length, axis=dim)
        leading = lax.slice_in_dim(shard, 0, width, axis=dim)
        before = lax.ppermute(last, axis, up)
        after = lax.ppermute(leading, axis, down)
        shard = jnp.concatenate([before, shard, after], axis=dim)
    return shard


def hamilton(field, potential):
    planes = field.shape[0]
    padded = padded_2(field, (("space", 0),), 4)
    laplace = 3.0 * STENCIL[0] * field
    for offset in range(1, 5):
        upper = padded[4 + offset : 4 + offset + planes]
        below = padded[4 - offset : 4 - offset + planes]
        laplace = laplace + STENCIL[offset] * (upper + below)
    for axis in (1, 2):
        for offset in range(1, 5):
            laplace = laplace + STENCIL[offset] * (
                jnp.roll(field, offset, axis) + jnp.roll(field, -offset, axis)
            )
    return -0.5 * laplace + potential[..., None] * field


def chebyshev(block, potential):
    before = block
    current = (hamilton(block, potential) - SHIFT_MID * block) / HALF_WIDTH
    for order in range(DEGREE - 1):
        following = 2.0 * (hamilton(current, potential) - SHIFT_MID * current) / HALF_WIDTH - before
        before, current = (current, following)
    return current


def per_device(orbitals, potential):
    highest = lax.Precision.HIGHEST
    filtered = chebyshev(orbitals, potential)
    planes, rows_y, rows_z, columns = filtered.shape
    local_points = planes * rows_y * rows_z
    points = local_points * lax.axis_size("space")
    panel_dev = PANEL // lax.axis_size("orb")
    flat = filtered.reshape(local_points, columns)
    panel_own = flat[:, :panel_dev]
    trailing = flat[:, panel_dev:]
    panel = lax.all_gather(panel_own, "orb", axis=1, tiled=True)
    coupling_part = jnp.dot(panel.T, trailing, precision=highest)
    gram_part = jnp.dot(panel.T, panel, precision=highest)
    gram_full, coupling = lax.psum((gram_part, coupling_part), "space")
    gram_full = gram_full / points
    coupling = coupling / points
    lower_factor = jnp.linalg.cholesky(gram_full)
    identity = jnp.eye(PANEL, dtype=jnp.float32)
    inverse = lax.linalg.triangular_solve(lower_factor, identity, left_side=True, lower=True)
    start = lax.axis_index("orb") * panel_dev
    own_rows = lax.dynamic_slice_in_dim(inverse, start, panel_dev, 0)
    ortho_own = jnp.dot(panel, own_rows.T, precision=highest)
    middle = jnp.dot(inverse, coupling, precision=highest)
    project = jnp.dot(inverse.T, middle, precision=highest)
    trailing_new = trailing - jnp.dot(panel, project, precision=highest)
    joined = jnp.concatenate([ortho_own, trailing_new], axis=1)
    return joined.reshape(planes, rows_y, rows_z, columns)


def solution(mesh):
    placed = (P("space", None, None, "orb"), P("space", None, None))
    return jax.shard_map(
        per_device,
        mesh=mesh,
        in_specs=placed,
        out_specs=P("space", None, None, "orb"),
        check_vma=False,
    )
```

profile of v0, /device:TPU:0, one launch (start us, length us, event | category | flops | bytes accessed | tf_op | source)
XLA Modules:
  0.0 514.7 jit_solution(1693416008679827727)
XLA Ops:
  21.2 13.6 %collective-permute-done.1 = f32[4,16,32,128]{3,2,1,0:T(8,128)S(1)} collective-permute-done((f32[4,16,32,128]{3,2,1,0:T(8,128)}, f32[4,16,32,128]{3,2,1,0:T(8,128)S(1)}, u32[]{:S(2)}, u32[]{:S(2)}) %collective-permute-start.1) | collective-permute-done | bytes 1048608 | tf_op jit(solution)/shard_map/ppermute | solution.py:20
  35.0 21.6 %collective-permute-done = f32[4,16,32,128]{3,2,1,0:T(8,128)S(1)} collective-permute-done((f32[4,16,32,128]{3,2,1,0:T(8,128)}, f32[4,16,32,128]{3,2,1,0:T(8,128)S(1)}, u32[]{:S(2)}, u32[]{:S(2)}) %collective-permute-start) | collective-permute-done | bytes 1048608 | tf_op jit(solution)/shard_map/ppermute | solution.py:21
  56.6 5.3 %broadcast_multiply_fusion.1 = (f32[4,16,32,128]{3,2,1,0:T(8,128)S(1)}, f32[4,16,32,128]{3,2,1,0:T(8,128)S(1)}) fusion(f32[4,16,32,128]{3,2,1,0:T(8,128)S(1)} %copy-done, f32[4,16,32]{2,1,0:T(8,128)S(1)} %copy-done.12, f32[4,16,4,128]{3,2,1,0:T(4,128)} %get-tuple-element.156, f32[4,16,28,128]{3,2,1,0:T(8,128)S(1)} %get-tuple-element.158, ...), kind=kLoop, calls=%fused_computation.211 | loop fusion | flops 15466496 | bytes 28319744 | tf_op jit(solution)/shard_map/div | solution.py:44
  72.9 22.7 %collective-permute-done.2 = f32[4,16,32,128]{3,2,1,0:T(8,128)S(1)} collective-permute-done((f32[4,16,32,128]{3,2,1,0:T(8,128)S(1)}, f32[4,16,32,128]{3,2,1,0:T(8,128)S(1)}, u32[]{:S(2)}, u32[]{:S(2)}) %collective-permute-start.2) | collective-permute-done | bytes 1048608 | tf_op jit(solution)/shard_map/ppermute | solution.py:21
  95.6 20.6 %collective-permute-done.3 = f32[4,16,32,128]{3,2,1,0:T(8,128)S(1)} collective-permute-done((f32[4,16,32,128]{3,2,1,0:T(8,128)S(1)}, f32[4,16,32,128]{3,2,1,0:T(8,128)S(1)}, u32[]{:S(2)}, u32[]{:S(2)}) %collective-permute-start.3) | collective-permute-done | bytes 1048608 | tf_op jit(solution)/shard_map/ppermute | solution.py:20
  117.2 6.9 %multiply_subtract_fusion.2 = f32[4,16,32,128]{3,2,1,0:T(8,128)S(1)} fusion(f32[4,16,32,128]{3,2,1,0:T(8,128)S(1)} %copy-done, f32[4,16,32,128]{3,2,1,0:T(8,128)S(1)} %get-tuple-element.24, f32[4,16,4,128]{3,2,1,0:T(4,128)} %get-tuple-element.122, f32[4,16,28,128]{3,2,1,0:T(8,128)S(1)} %get-tuple-element.124, f32[4,16,28,128]{3,2,1,0:T(8,128)S(1)} %get-tuple-element.123, ...), kind=kLoop, calls=%fused_computation.201 | loop fusion | flops 17301504 | bytes 23076864 | tf_op jit(solution)/shard_map/sub | solution.py:46
  135.1 17.0 %collective-permute-done.4 = f32[4,16,32,128]{3,2,1,0:T(8,128)S(1)} collective-permute-done((f32[4,16,32,128]{3,2,1,0:T(8,128)S(1)}, f32[4,16,32,128]{3,2,1,0:T(8,128)S(1)}, u32[]{:S(2)}, u32[]{:S(2)}) %collective-permute-start.4) | collective-permute-done | bytes 1048608 | tf_op jit(solution)/shard_map/ppermute | solution.py:21
  152.1 20.4 %collective-permute-done.5 = f32[4,16,32,128]{3,2,1,0:T(8,128)S(1)} collective-permute-done((f32[4,16,32,128]{3,2,1,0:T(8,128)S(1)}, f32[4,16,32,128]{3,2,1,0:T(8,128)S(1)}, u32[]{:S(2)}, u32[]{:S(2)}) %collective-permute-start.5) | collective-permute-done | bytes 1048608 | tf_op jit(solution)/shard_map/ppermute | solution.py:20
  173.5 6.9 %multiply_subtract_fusion.1 = f32[4,16,32,128]{3,2,1,0:T(8,128)S(1)} fusion(f32[4,16,32,128]{3,2,1,0:T(8,128)S(1)} %multiply_subtract_fusion.2, f32[4,16,4,128]{3,2,1,0:T(4,128)} %get-tuple-element.90, f32[4,16,28,128]{3,2,1,0:T(8,128)S(1)} %get-tuple-element.92, f32[4,16,28,128]{3,2,1,0:T(8,128)S(1)} %get-tuple-element.91, ...), kind=kLoop, calls=%fused_computation.200 | loop fusion | flops 17563648 | bytes 22028288 | tf_op jit(solution)/shard_map/sub | solution.py:46
  190.4 18.2 %collective-permute-done.6 = f32[4,16,32,128]{3,2,1,0:T(8,128)S(1)} collective-permute-done((f32[4,16,32,128]{3,2,1,0:T(8,128)S(1)}, f32[4,16,32,128]{3,2,1,0:T(8,128)S(1)}, u32[]{:S(2)}, u32[]{:S(2)}) %collective-permute-start.6) | collective-permute-done | bytes 1048608 | tf_op jit(solution)/shard_map/ppermute | solution.py:21
  208.7 19.4 %collective-permute-done.7 = f32[4,16,32,128]{3,2,1,0:T(8,128)S(1)} collective-permute-done((f32[4,16,32,128]{3,2,1,0:T(8,128)S(1)}, f32[4,16,32,128]{3,2,1,0:T(8,128)S(1)}, u32[]{:S(2)}, u32[]{:S(2)}) %collective-permute-start.7) | collective-permute-done | bytes 1048608 | tf_op jit(solution)/shard_map/ppermute | solution.py:20
  229.1 6.8 %multiply_subtract_fusion = f32[4,16,32,128]{3,2,1,0:T(8,128)S(1)} fusion(f32[4,16,32,128]{3,2,1,0:T(8,128)S(1)} %multiply_subtract_fusion.2, f32[4,16,32,128]{3,2,1,0:T(8,128)S(1)} %multiply_subtract_fusion.1, f32[4,16,4,128]{3,2,1,0:T(4,128)} %get-tuple-element.58, f32[4,16,28,128]{3,2,1,0:T(8,128)S(1)} %get-tuple-element.60, ...), kind=kLoop, calls=%fused_computation.199 | loop fusion | flops 17301504 | bytes 22028288 | tf_op jit(solution)/shard_map/sub | solution.py:46
  237.5 47.5 %all-gather.2.cloned.1.call-done = f32[2048,512]{0,1:T(8,128)} async-done(((f32[2048,64]{0,1:T(8,128)}), f32[2048,512]{0,1:T(8,128)}) %all-gather.2.cloned.1.call-update) | async-done | bytes 4194320 | tf_op jit(solution)/shard_map/all_gather | solution.py:61
  285.0 10.7 %fusion.224 = f32[512,512]{0,1:T(8,128)} fusion(f32[2048,512]{0,1:T(8,128)} %all-gather.2.cloned.1.call-done), kind=kOutput, calls=%fused_computation.337 | convolution fusion | flops 6442450944 | bytes 5242880 | tf_op jit(solution)/shard_map/dot_general | solution.py:63
  303.0 51.0 %all-reduce.4.cloned.1.call-done = (f32[512,64]{0,1:T(8,128)}, f32[512,512]{0,1:T(8,128)}) async-done(((f32[512,64]{0,1:T(8,128)}, f32[512,512]{0,1:T(8,128)}), (f32[512,64]{0,1:T(8,128)}, f32[512,512]{0,1:T(8,128)})) %all-reduce.4.cloned.1.call-update) | async-done | bytes 1179664 | tf_op jit(solution)/shard_map/psum | solution.py:64
  356.0 11.7 %cholesky.104 = f32[128,128]{1,0:T(8,128)S(1)} custom-call(f32[128,128]{1,0:T(8,128)S(1)} %cholesky.266), custom_call_target="Cholesky" | custom-call | tf_op jit(solution)/shard_map/jit(cholesky)/cholesky | solution.py:67
  367.9 9.8 %custom-call.30 = f32[1,128,128]{1,2,0:T(8,128)S(1)} custom-call(f32[1,128,128]{2,1,0:T(8,128)S(1)} %get-tuple-element.168), custom_call_target="InvertDiagBlocksLowerTriangular" | custom-call | tf_op jit(solution)/shard_map/jit(cholesky)/cholesky | solution.py:67
  378.4 11.9 %cholesky.217 = f32[128,128]{1,0:T(8,128)S(1)} custom-call(f32[128,128]{1,0:T(8,128)S(1)} %cholesky.270), custom_call_target="Cholesky" | custom-call | tf_op jit(solution)/shard_map/jit(cholesky)/cholesky | solution.py:67
  390.3 9.8 %custom-call.31 = f32[1,128,128]{1,2,0:T(8,128)S(1)} custom-call(f32[1,128,128]{2,1,0:T(8,128)S(1)} %get-tuple-element.165), custom_call_target="InvertDiagBlocksLowerTriangular" | custom-call | tf_op jit(solution)/shard_map/jit(cholesky)/cholesky | solution.py:67
  400.8 12.3 %cholesky.238 = f32[128,128]{1,0:T(8,128)} custom-call(f32[128,128]{1,0:T(8,128)S(1)} %cholesky.275), custom_call_target="Cholesky" | custom-call | tf_op jit(solution)/shard_map/jit(cholesky)/cholesky | solution.py:67
  415.4 11.3 %custom-call.32 = f32[1,128,128]{1,2,0:T(8,128)} custom-call(f32[1,128,128]{2,1,0:T(8,128)} %get-tuple-element.162), custom_call_target="InvertDiagBlocksLowerTriangular" | custom-call | tf_op jit(solution)/shard_map/jit(cholesky)/cholesky | solution.py:67
  428.1 11.9 %cholesky.255 = f32[128,128]{1,0:T(8,128)S(1)} custom-call(f32[128,128]{1,0:T(8,128)S(1)} %convolution_subtract_fusion.6), custom_call_target="Cholesky" | custom-call | tf_op jit(solution)/shard_map/jit(cholesky)/cholesky | solution.py:67
  444.2 10.8 %while.1 = (s32[]{:T(128)}, f32[512,512]{1,0:T(8,128)S(1)}, s32[4,2]{0,1:T(2,128)S(1)}, f32[4,128,128]{2,1,0:T(8,128)}, s32[]{:T(128)}) while((s32[]{:T(128)}, f32[512,512]{1,0:T(8,128)S(1)}, s32[4,2]{0,1:T(2,128)S(1)}, f32[4,128,128]{2,1,0:T(8,128)}, s32[]{:T(128)}) %tuple.94), condition=%wide.while_cond, body=%wide.while_body.sunk | while | flops 2 | bytes 132705 | solution.py:69
  455.0 40.1 %custom-call.33 = f32[4,128,128]{1,2,0:T(8,128)S(1)} custom-call(f32[4,128,128]{2,1,0:T(8,128)} %get-tuple-element.12), custom_call_target="InvertDiagBlocksLowerTriangular" | custom-call | tf_op jit(solution)/shard_map/triangular_solve | solution.py:69
  (166 shorter events, 90.2 us)
Async XLA Ops:
  6.5 5.8 %copy-start = (f32[4,16,32,128]{3,2,1,0:T(8,128)S(1)}, f32[4,16,32,128]{3,2,1,0:T(8,128)}, u32[]{:S(2)}) copy-start(f32[4,16,32,128]{3,2,1,0:T(8,128)} %param.2) | copy-start | bytes 3145732
  6.5 278.4 %all-gather.2.cloned.1.call-start = ((), (), s32[]{:S(2)}) async-start(), calls=%async_computation | async-start | bytes 4718592 | tf_op jit(solution)/shard_map/all_gather | solution.py:61
  6.5 28.2 %collective-permute-start.1 = (f32[4,16,32,128]{3,2,1,0:T(8,128)}, f32[4,16,32,128]{3,2,1,0:T(8,128)S(1)}, u32[]{:S(2)}, u32[]{:S(2)}) collective-permute-start(f32[4,16,32,128]{3,2,1,0:T(8,128)} %param.2), channel_id=1, source_target_pairs={{0,8},{8,16},{16,24},{24,0},{1,9},{9,17},{17,25},{25,1},{2,10},{10... | collective-permute-start | bytes 3145736 | tf_op jit(solution)/shard_map/ppermute | solution.py:20
  9.5 47.0 %collective-permute-start = (f32[4,16,32,128]{3,2,1,0:T(8,128)}, f32[4,16,32,128]{3,2,1,0:T(8,128)S(1)}, u32[]{:S(2)}, u32[]{:S(2)}) collective-permute-start(f32[4,16,32,128]{3,2,1,0:T(8,128)} %param.2), channel_id=1, source_target_pairs={{8,0},{16,8},{24,16},{0,24},{9,1},{17,9},{25,17},{1,25},{10,2},{18... | collective-permute-start | bytes 3145736 | tf_op jit(solution)/shard_map/ppermute | solution.py:21
  16.4 4.3 copy-start.12
  69.5 26.0 %collective-permute-start.2 = (f32[4,16,32,128]{3,2,1,0:T(8,128)S(1)}, f32[4,16,32,128]{3,2,1,0:T(8,128)S(1)}, u32[]{:S(2)}, u32[]{:S(2)}) collective-permute-start(f32[4,16,32,128]{3,2,1,0:T(8,128)S(1)} %get-tuple-element.23), channel_id=1, source_target_pairs={{8,0},{16,8},{24,16},{0,24},{9,1},{17,9},{25,17},{1,25},{10,2},{18... | collective-permute-start | bytes 3145736 | tf_op jit(solution)/shard_map/ppermute | solution.py:21
  71.0 45.2 %collective-permute-start.3 = (f32[4,16,32,128]{3,2,1,0:T(8,128)S(1)}, f32[4,16,32,128]{3,2,1,0:T(8,128)S(1)}, u32[]{:S(2)}, u32[]{:S(2)}) collective-permute-start(f32[4,16,32,128]{3,2,1,0:T(8,128)S(1)} %get-tuple-element.23), channel_id=1, source_target_pairs={{0,8},{8,16},{16,24},{24,0},{1,9},{9,17},{17,25},{25,1},{2,10},{10... | collective-permute-start | bytes 3145736 | tf_op jit(solution)/shard_map/ppermute | solution.py:20
  95.6 20.6 %copy-start.10 = (f32[4,16,32,128]{3,2,1,0:T(8,128)}, f32[4,16,32,128]{3,2,1,0:T(8,128)S(1)}, u32[]{:S(2)}) copy-start(f32[4,16,32,128]{3,2,1,0:T(8,128)S(1)} %collective-permute-done.2) | copy-start | bytes 3145732
  116.2 1.0 copy-start.11
  126.0 26.0 %collective-permute-start.4 = (f32[4,16,32,128]{3,2,1,0:T(8,128)S(1)}, f32[4,16,32,128]{3,2,1,0:T(8,128)S(1)}, u32[]{:S(2)}, u32[]{:S(2)}) collective-permute-start(f32[4,16,32,128]{3,2,1,0:T(8,128)S(1)} %multiply_subtract_fusion.2), channel_id=1, source_target_pairs={{8,0},{16,8},{24,16},{0,24},{9,1},{17,9},{25,17},{1,25},{10,2},{18... | collective-permute-start | bytes 3145736 | tf_op jit(solution)/shard_map/ppermute | solution.py:21
  128.3 44.2 %collective-permute-start.5 = (f32[4,16,32,128]{3,2,1,0:T(8,128)S(1)}, f32[4,16,32,128]{3,2,1,0:T(8,128)S(1)}, u32[]{:S(2)}, u32[]{:S(2)}) collective-permute-start(f32[4,16,32,128]{3,2,1,0:T(8,128)S(1)} %multiply_subtract_fusion.2), channel_id=1, source_target_pairs={{0,8},{8,16},{16,24},{24,0},{1,9},{9,17},{17,25},{25,1},{2,10},{10... | collective-permute-start | bytes 3145736 | tf_op jit(solution)/shard_map/ppermute | solution.py:20
  152.1 20.4 %copy-start.7 = (f32[4,16,32,128]{3,2,1,0:T(8,128)}, f32[4,16,32,128]{3,2,1,0:T(8,128)S(1)}, u32[]{:S(2)}) copy-start(f32[4,16,32,128]{3,2,1,0:T(8,128)S(1)} %collective-permute-done.4) | copy-start | bytes 3145732
  172.5 1.0 copy-start.9
  182.6 26.0 %collective-permute-start.6 = (f32[4,16,32,128]{3,2,1,0:T(8,128)S(1)}, f32[4,16,32,128]{3,2,1,0:T(8,128)S(1)}, u32[]{:S(2)}, u32[]{:S(2)}) collective-permute-start(f32[4,16,32,128]{3,2,1,0:T(8,128)S(1)} %multiply_subtract_fusion.1), channel_id=1, source_target_pairs={{8,0},{16,8},{24,16},{0,24},{9,1},{17,9},{25,17},{1,25},{10,2},{18... | collective-permute-start | bytes 3145736 | tf_op jit(solution)/shard_map/ppermute | solution.py:21
  184.1 44.0 %collective-permute-start.7 = (f32[4,16,32,128]{3,2,1,0:T(8,128)S(1)}, f32[4,16,32,128]{3,2,1,0:T(8,128)S(1)}, u32[]{:S(2)}, u32[]{:S(2)}) collective-permute-start(f32[4,16,32,128]{3,2,1,0:T(8,128)S(1)} %multiply_subtract_fusion.1), channel_id=1, source_target_pairs={{0,8},{8,16},{16,24},{24,0},{1,9},{9,17},{17,25},{25,1},{2,10},{10... | collective-permute-start | bytes 3145736 | tf_op jit(solution)/shard_map/ppermute | solution.py:20
  190.2 38.9 %copy-start.13 = (f32[4,16,32]{2,1,0:T(8,128)S(1)}, f32[4,16,32]{2,1,0:T(8,128)}, u32[]{:S(2)}) copy-start(f32[4,16,32]{2,1,0:T(8,128)} %param.3) | copy-start | bytes 24580
  208.7 19.4 %copy-start.6 = (f32[4,16,32,128]{3,2,1,0:T(8,128)}, f32[4,16,32,128]{3,2,1,0:T(8,128)S(1)}, u32[]{:S(2)}) copy-start(f32[4,16,32,128]{3,2,1,0:T(8,128)S(1)} %collective-permute-done.6) | copy-start | bytes 3145732
  237.4 116.6 %all-reduce.4.cloned.1.call-start = ((), (), s32[]{:S(2)}) async-start(), calls=%async_computation.1 | async-start | bytes 2359296 | tf_op jit(solution)/shard_map/psum | solution.py:64
  285.0 10.7 %copy-start.1 = (f32[2048,512]{0,1:T(8,128)S(1)}, f32[2048,512]{0,1:T(8,128)}, u32[]{:S(2)}) copy-start(f32[2048,512]{0,1:T(8,128)} %all-gather.2.cloned.1.call-done) | copy-start | bytes 12582916
  354.0 1.8 copy-start.3
  413.1 82.3 %copy-start.4 = (f32[512,512]{1,0:T(8,128)S(1)}, f32[512,512]{1,0:T(8,128)}, u32[]{:S(2)}) copy-start(f32[512,512]{1,0:T(8,128)} %fusion.125) | copy-start | bytes 3145732
  497.1 1.2 copy-start.14
  498.2 2.2 copy-start.2
  500.4 2.9 copy-start.5
  (1 other events, 1.0 us)
Sparse Core Ops, SparseCore 0:
  237.5 47.3 all-gather.1
  300.8 53.1 all-reduce.3
where the time goes:
time: 522 us; the launch traced here: 515 us
  waiting for transfers between devices  252 us (48%)
  other arithmetic  152 us (29%)
  local copies, waits for them, and re-layouts  54.5 us (10%)
  matrix products  29 us (6%)
  between operations  17 us (3%)
  starting transfers between devices  10.5 us (2%)
    another operation x14, other arithmetic, per_device(): lower_factor = jnp.linalg.cholesky(gram_full)  82.5 us
    ppermute x4, waiting for transfers between devices, padded_2(): after = lax.ppermute(leading, axis, down)  79.4 us
    ppermute x4, waiting for transfers between devices, padded_2(): before = lax.ppermute(last, axis, up)  74 us
    psum x1, waiting for transfers between devices, per_device(): gram_full, coupling = lax.psum((gram_part, coupling_part), 'space')  51 us
    all_gather x1, waiting for transfers between devices, per_device(): panel = lax.all_gather(panel_own, 'orb', axis=1, tiled=True)  47.5 us
    another operation x4, other arithmetic, per_device(): lax.linalg.triangular_solve(lower_factor, identity, left_side=True, lower...  40.3 us
    slice x64, local copies, waits for them, and re-layouts, hamilton(): jnp.roll(field, offset, axis) + jnp.roll(field, -offset, axis)  35.9 us
    sub x3, other arithmetic, chebyshev(): 2.0 * (hamilton(current, potential) - SHIFT_MID * current) / HALF_WIDTH  20.7 us
  transfers between devices with their start and end apart: 10, of which 10 were waited for; matrix products, arithmetic and copies ran while one was open for 5% of the time, Pallas kernels for 0%

commit v1 on v0

--- a/solution.py
+++ b/solution.py
@@ -58,7 +58,14 @@
     flat = filtered.reshape(local_points, columns)
     panel_own = flat[:, :panel_dev]
     trailing = flat[:, panel_dev:]
-    panel = lax.all_gather(panel_own, "orb", axis=1, tiled=True)
+    ways, here, step = (lax.axis_size("orb"), lax.axis_index("orb"), panel_own.shape[1])
+    line, have = (panel_own, 1)
+    while have < ways:
+        line = jnp.concatenate(
+            [line, lax.ppermute(line, "orb", [(d, (d - have) % ways) for d in range(ways)])], axis=1
+        )
+        have = 2 * have
+    panel = jnp.roll(line, here * step, axis=1)
     coupling_part = jnp.dot(panel.T, trailing, precision=highest)
     gram_part = jnp.dot(panel.T, panel, precision=highest)
     gram_full, coupling = lax.psum((gram_part, coupling_part), "space")

time: 522 us -> 626 us (1.20)
  waiting for transfers between devices: 252 us -> 329 us
  local copies, waits for them, and re-layouts: 54.5 us -> 65.3 us
  matrix products: 29 us -> 38.8 us
    ppermute x0 -> x3, waiting for transfers between devices: none -> 123 us  [per_device(): lax.ppermute(line, 'orb', [(d, (d - have) % ways) for d in range(ways)])]
    all_gather x1 -> x0, waiting for transfers between devices: 47.5 us -> none  [per_device(): panel = lax.all_gather(panel_own, 'orb', axis=1, tiled=True)]
    concatenate x0 -> x1, local copies, waits for them, and re-layouts: none -> 9.97 us  [per_device(): panel = jnp.roll(line, here * step, axis=1)]
  transfers between devices with their start and end apart: 10 -> 12, of which waited for: 10 -> 12; matrix products, arithmetic and copies ran while one was open for 5% -> 4% of each run, Pallas kernels for 0% -> 0%
where the time goes in v1:
time: 626 us; the launch traced here: 618 us
  waiting for transfers between devices  329 us (53%)
  other arithmetic  154 us (25%)
  local copies, waits for them, and re-layouts  65.3 us (10%)
  matrix products  38.8 us (6%)
  between operations  17 us (3%)
  starting transfers between devices  14.3 us (2%)
    ppermute x3, waiting for transfers between devices, per_device(): lax.ppermute(line, 'orb', [(d, (d - have) % ways) for d in range(ways)])  123 us
    another operation x14, other arithmetic, per_device(): lower_factor = jnp.linalg.cholesky(gram_full)  82.4 us
    ppermute x4, waiting for transfers between devices, padded_2(): after = lax.ppermute(leading, axis, down)  79.4 us
    ppermute x4, waiting for transfers between devices, padded_2(): before = lax.ppermute(last, axis, up)  74 us
    psum x1, waiting for transfers between devices, per_device(): gram_full, coupling = lax.psum((gram_part, coupling_part), 'space')  52.4 us
    another operation x4, other arithmetic, per_device(): lax.linalg.triangular_solve(lower_factor, identity, left_side=True, lower...  40.3 us
    slice x64, local copies, waits for them, and re-layouts, hamilton(): jnp.roll(field, offset, axis) + jnp.roll(field, -offset, axis)  35.9 us
    sub x3, other arithmetic, chebyshev(): 2.0 * (hamilton(current, potential) - SHIFT_MID * current) / HALF_WIDTH  20.7 us
  transfers between devices with their start and end apart: 12, of which 12 were waited for; matrix products, arithmetic and copies ran while one was open for 4% of the time, Pallas kernels for 0%

profile of v1, /device:TPU:0, one launch (start us, length us, event | category | flops | bytes accessed | tf_op | source)
XLA Modules:
  0.0 618.4 jit_solution(2240156497711640495)
XLA Ops:
  21.2 13.6 %collective-permute-done.1 = f32[4,16,32,128]{3,2,1,0:T(8,128)S(1)} collective-permute-done((f32[4,16,32,128]{3,2,1,0:T(8,128)}, f32[4,16,32,128]{3,2,1,0:T(8,128)S(1)}, u32[]{:S(2)}, u32[]{:S(2)}) %collective-permute-start.1) | collective-permute-done | bytes 1048608 | tf_op jit(solution)/shard_map/ppermute | solution.py:20
  35.0 21.6 %collective-permute-done = f32[4,16,32,128]{3,2,1,0:T(8,128)S(1)} collective-permute-done((f32[4,16,32,128]{3,2,1,0:T(8,128)}, f32[4,16,32,128]{3,2,1,0:T(8,128)S(1)}, u32[]{:S(2)}, u32[]{:S(2)}) %collective-permute-start) | collective-permute-done | bytes 1048608 | tf_op jit(solution)/shard_map/ppermute | solution.py:21
  72.9 22.7 %collective-permute-done.2 = f32[4,16,32,128]{3,2,1,0:T(8,128)S(1)} collective-permute-done((f32[4,16,32,128]{3,2,1,0:T(8,128)S(1)}, f32[4,16,32,128]{3,2,1,0:T(8,128)S(1)}, u32[]{:S(2)}, u32[]{:S(2)}) %collective-permute-start.2) | collective-permute-done | bytes 1048608 | tf_op jit(solution)/shard_map/ppermute | solution.py:21
  95.6 20.6 %collective-permute-done.3 = f32[4,16,32,128]{3,2,1,0:T(8,128)S(1)} collective-permute-done((f32[4,16,32,128]{3,2,1,0:T(8,128)S(1)}, f32[4,16,32,128]{3,2,1,0:T(8,128)S(1)}, u32[]{:S(2)}, u32[]{:S(2)}) %collective-permute-start.3) | collective-permute-done | bytes 1048608 | tf_op jit(solution)/shard_map/ppermute | solution.py:20
  117.2 6.9 %multiply_subtract_fusion.2 = f32[4,16,32,128]{3,2,1,0:T(8,128)S(1)} fusion(f32[4,16,32,128]{3,2,1,0:T(8,128)S(1)} %copy-done, f32[4,16,32,128]{3,2,1,0:T(8,128)S(1)} %get-tuple-element.24, f32[4,16,4,128]{3,2,1,0:T(4,128)} %get-tuple-element.122, f32[4,16,28,128]{3,2,1,0:T(8,128)S(1)} %get-tuple-element.124, f32[4,16,28,128]{3,2,1,0:T(8,128)S(1)} %get-tuple-element.123, ...), kind=kLoop, calls=%fused_computation.211 | loop fusion | flops 17301504 | bytes 23076864 | tf_op jit(solution)/shard_map/sub | solution.py:46
  135.1 17.0 %collective-permute-done.4 = f32[4,16,32,128]{3,2,1,0:T(8,128)S(1)} collective-permute-done((f32[4,16,32,128]{3,2,1,0:T(8,128)S(1)}, f32[4,16,32,128]{3,2,1,0:T(8,128)S(1)}, u32[]{:S(2)}, u32[]{:S(2)}) %collective-permute-start.4) | collective-permute-done | bytes 1048608 | tf_op jit(solution)/shard_map/ppermute | solution.py:21
  152.1 20.4 %collective-permute-done.5 = f32[4,16,32,128]{3,2,1,0:T(8,128)S(1)} collective-permute-done((f32[4,16,32,128]{3,2,1,0:T(8,128)S(1)}, f32[4,16,32,128]{3,2,1,0:T(8,128)S(1)}, u32[]{:S(2)}, u32[]{:S(2)}) %collective-permute-start.5) | collective-permute-done | bytes 1048608 | tf_op jit(solution)/shard_map/ppermute | solution.py:20
  173.5 7.0 %multiply_subtract_fusion.1 = f32[4,16,32,128]{3,2,1,0:T(8,128)S(1)} fusion(f32[4,16,32,128]{3,2,1,0:T(8,128)S(1)} %multiply_subtract_fusion.2, f32[4,16,4,128]{3,2,1,0:T(4,128)} %get-tuple-element.90, f32[4,16,28,128]{3,2,1,0:T(8,128)S(1)} %get-tuple-element.92, f32[4,16,28,128]{3,2,1,0:T(8,128)S(1)} %get-tuple-element.91, ...), kind=kLoop, calls=%fused_computation.210 | loop fusion | flops 17563648 | bytes 22028288 | tf_op jit(solution)/shard_map/sub | solution.py:46
  190.5 18.3 %collective-permute-done.6 = f32[4,16,32,128]{3,2,1,0:T(8,128)S(1)} collective-permute-done((f32[4,16,32,128]{3,2,1,0:T(8,128)S(1)}, f32[4,16,32,128]{3,2,1,0:T(8,128)S(1)}, u32[]{:S(2)}, u32[]{:S(2)}) %collective-permute-start.6) | collective-permute-done | bytes 1048608 | tf_op jit(solution)/shard_map/ppermute | solution.py:21
  208.7 19.4 %collective-permute-done.7 = f32[4,16,32,128]{3,2,1,0:T(8,128)S(1)} collective-permute-done((f32[4,16,32,128]{3,2,1,0:T(8,128)S(1)}, f32[4,16,32,128]{3,2,1,0:T(8,128)S(1)}, u32[]{:S(2)}, u32[]{:S(2)}) %collective-permute-start.7) | collective-permute-done | bytes 1048608 | tf_op jit(solution)/shard_map/ppermute | solution.py:20
  249.0 23.2 %collective-permute-done.9 = f32[2048,128]{1,0:T(8,128)S(1)} collective-permute-done((f32[2048,128]{1,0:T(8,128)S(1)}, f32[2048,128]{1,0:T(8,128)S(1)}, u32[]{:S(2)}, u32[]{:S(2)}) %collective-permute-start.9) | collective-permute-done | bytes 1048608 | tf_op jit(solution)/shard_map/ppermute | solution.py:65
  275.0 93.3 %collective-permute-done.10 = f32[2048,256]{1,0:T(8,128)} collective-permute-done((f32[2048,256]{1,0:T(8,128)}, f32[2048,256]{1,0:T(8,128)}, u32[]{:S(2)}, u32[]{:S(2)}) %collective-permute-start.10) | collective-permute-done | bytes 2097184 | tf_op jit(solution)/shard_map/ppermute | solution.py:65
  368.3 10.0 %concatenate.351 = f32[2048,1024]{1,0:T(8,128)} concatenate(f32[2048,64]{1,0:T(8,128)S(1)} %get-tuple-element.27, f32[2048,64]{1,0:T(8,128)S(1)} %copy.14, f32[2048,128]{1,0:T(8,128)} %copy-done.1, f32[2048,256]{1,0:T(8,128)} %collective-permute-done.10, f32[2048,64]{1,0:T(8,128)S(1)} %get-tuple-element.27, f32[2048,64]{1,0:T(8,128)S(1)} %copy.14, f32[2048,128]{1,0:T(8,128)} %copy-done.1, ...), dimensions={1} | concatenate | bytes 16777216 | tf_op jit(solution)/shard_map/jit(_roll_dynamic)/concatenate | solution.py:68
  378.3 13.6 %fusion.6 = f32[512,512]{0,1:T(8,128)} fusion(f32[2048,1024]{1,0:T(8,128)} %concatenate.351, s32[]{:T(128)S(6)} %select_n.21), kind=kOutput, calls=%fused_computation.8 | convolution fusion | flops 6442450944 | bytes 5242884 | tf_op jit(solution)/shard_map/dot_general | solution.py:70
  400.6 52.4 %all-reduce.4.cloned.1.call-done = (f32[512,64]{0,1:T(8,128)}, f32[512,512]{0,1:T(8,128)}) async-done(((f32[512,64]{0,1:T(8,128)}, f32[512,512]{0,1:T(8,128)}), (f32[512,64]{0,1:T(8,128)}, f32[512,512]{0,1:T(8,128)})) %all-reduce.4.cloned.1.call-update) | async-done | bytes 1179664 | tf_op jit(solution)/shard_map/psum | solution.py:71
  455.0 11.7 %cholesky.104 = f32[128,128]{1,0:T(8,128)S(1)} custom-call(f32[128,128]{1,0:T(8,128)S(1)} %cholesky.266), custom_call_target="Cholesky" | custom-call | tf_op jit(solution)/shard_map/jit(cholesky)/cholesky | solution.py:74
  466.9 9.8 %custom-call.30 = f32[1,128,128]{1,2,0:T(8,128)S(1)} custom-call(f32[1,128,128]{2,1,0:T(8,128)S(1)} %get-tuple-element.168), custom_call_target="InvertDiagBlocksLowerTriangular" | custom-call | tf_op jit(solution)/shard_map/jit(cholesky)/cholesky | solution.py:74
  477.4 11.9 %cholesky.217 = f32[128,128]{1,0:T(8,128)S(1)} custom-call(f32[128,128]{1,0:T(8,128)S(1)} %cholesky.270), custom_call_target="Cholesky" | custom-call | tf_op jit(solution)/shard_map/jit(cholesky)/cholesky | solution.py:74
  489.3 9.8 %custom-call.31 = f32[1,128,128]{1,2,0:T(8,128)S(1)} custom-call(f32[1,128,128]{2,1,0:T(8,128)S(1)} %get-tuple-element.165), custom_call_target="InvertDiagBlocksLowerTriangular" | custom-call | tf_op jit(solution)/shard_map/jit(cholesky)/cholesky | solution.py:74
  499.8 12.3 %cholesky.238 = f32[128,128]{1,0:T(8,128)} custom-call(f32[128,128]{1,0:T(8,128)S(1)} %cholesky.275), custom_call_target="Cholesky" | custom-call | tf_op jit(solution)/shard_map/jit(cholesky)/cholesky | solution.py:74
  514.3 11.3 %custom-call.32 = f32[1,128,128]{1,2,0:T(8,128)} custom-call(f32[1,128,128]{2,1,0:T(8,128)} %get-tuple-element.162), custom_call_target="InvertDiagBlocksLowerTriangular" | custom-call | tf_op jit(solution)/shard_map/jit(cholesky)/cholesky | solution.py:74
  527.0 11.9 %cholesky.255 = f32[128,128]{1,0:T(8,128)S(1)} custom-call(f32[128,128]{1,0:T(8,128)S(1)} %convolution_subtract_fusion.5), custom_call_target="Cholesky" | custom-call | tf_op jit(solution)/shard_map/jit(cholesky)/cholesky | solution.py:74
  543.0 10.2 %while.1 = (s32[]{:T(128)}, f32[512,512]{1,0:T(8,128)S(1)}, s32[4,2]{0,1:T(2,128)S(1)}, f32[4,128,128]{2,1,0:T(8,128)}, s32[]{:T(128)}) while((s32[]{:T(128)}, f32[512,512]{1,0:T(8,128)S(1)}, s32[4,2]{0,1:T(2,128)S(1)}, f32[4,128,128]{2,1,0:T(8,128)}, s32[]{:T(128)}) %tuple.94), condition=%wide.while_cond, body=%wide.while_body.sunk | while | flops 2 | bytes 132705 | solution.py:76
  553.2 40.1 %custom-call.33 = f32[4,128,128]{1,2,0:T(8,128)S(1)} custom-call(f32[4,128,128]{2,1,0:T(8,128)} %get-tuple-element.12), custom_call_target="InvertDiagBlocksLowerTriangular" | custom-call | tf_op jit(solution)/shard_map/triangular_solve | solution.py:76
  (178 shorter events, 122.8 us)
Async XLA Ops:
  6.5 5.8 copy-start
  6.5 446.4 %all-reduce.4.cloned.1.call-start = ((), (), s32[]{:S(2)}) async-start(), calls=%async_computation | async-start | bytes 2359296 | tf_op jit(solution)/shard_map/psum | solution.py:71
  6.5 28.2 %collective-permute-start.1 = (f32[4,16,32,128]{3,2,1,0:T(8,128)}, f32[4,16,32,128]{3,2,1,0:T(8,128)S(1)}, u32[]{:S(2)}, u32[]{:S(2)}) collective-permute-start(f32[4,16,32,128]{3,2,1,0:T(8,128)} %param.2), channel_id=1, source_target_pairs={{0,8},{8,16},{16,24},{24,0},{1,9},{9,17},{17,25},{25,1},{2,10},{10... | collective-permute-start | bytes 3145736 | tf_op jit(solution)/shard_map/ppermute | solution.py:20
  9.5 47.0 %collective-permute-start = (f32[4,16,32,128]{3,2,1,0:T(8,128)}, f32[4,16,32,128]{3,2,1,0:T(8,128)S(1)}, u32[]{:S(2)}, u32[]{:S(2)}) collective-permute-start(f32[4,16,32,128]{3,2,1,0:T(8,128)} %param.2), channel_id=1, source_target_pairs={{8,0},{16,8},{24,16},{0,24},{9,1},{17,9},{25,17},{1,25},{10,2},{18... | collective-permute-start | bytes 3145736 | tf_op jit(solution)/shard_map/ppermute | solution.py:21
  16.4 4.3 copy-start.12
  69.6 26.0 %collective-permute-start.2 = (f32[4,16,32,128]{3,2,1,0:T(8,128)S(1)}, f32[4,16,32,128]{3,2,1,0:T(8,128)S(1)}, u32[]{:S(2)}, u32[]{:S(2)}) collective-permute-start(f32[4,16,32,128]{3,2,1,0:T(8,128)S(1)} %get-tuple-element.23), channel_id=1, source_target_pairs={{8,0},{16,8},{24,16},{0,24},{9,1},{17,9},{25,17},{1,25},{10,2},{18... | collective-permute-start | bytes 3145736 | tf_op jit(solution)/shard_map/ppermute | solution.py:21
  71.0 45.2 %collective-permute-start.3 = (f32[4,16,32,128]{3,2,1,0:T(8,128)S(1)}, f32[4,16,32,128]{3,2,1,0:T(8,128)S(1)}, u32[]{:S(2)}, u32[]{:S(2)}) collective-permute-start(f32[4,16,32,128]{3,2,1,0:T(8,128)S(1)} %get-tuple-element.23), channel_id=1, source_target_pairs={{0,8},{8,16},{16,24},{24,0},{1,9},{9,17},{17,25},{25,1},{2,10},{10... | collective-permute-start | bytes 3145736 | tf_op jit(solution)/shard_map/ppermute | solution.py:20
  95.6 20.6 %copy-start.10 = (f32[4,16,32,128]{3,2,1,0:T(8,128)}, f32[4,16,32,128]{3,2,1,0:T(8,128)S(1)}, u32[]{:S(2)}) copy-start(f32[4,16,32,128]{3,2,1,0:T(8,128)S(1)} %collective-permute-done.2) | copy-start | bytes 3145732
  126.0 26.0 %collective-permute-start.4 = (f32[4,16,32,128]{3,2,1,0:T(8,128)S(1)}, f32[4,16,32,128]{3,2,1,0:T(8,128)S(1)}, u32[]{:S(2)}, u32[]{:S(2)}) collective-permute-start(f32[4,16,32,128]{3,2,1,0:T(8,128)S(1)} %multiply_subtract_fusion.2), channel_id=1, source_target_pairs={{8,0},{16,8},{24,16},{0,24},{9,1},{17,9},{25,17},{1,25},{10,2},{18... | collective-permute-start | bytes 3145736 | tf_op jit(solution)/shard_map/ppermute | solution.py:21
  128.3 44.2 %collective-permute-start.5 = (f32[4,16,32,128]{3,2,1,0:T(8,128)S(1)}, f32[4,16,32,128]{3,2,1,0:T(8,128)S(1)}, u32[]{:S(2)}, u32[]{:S(2)}) collective-permute-start(f32[4,16,32,128]{3,2,1,0:T(8,128)S(1)} %multiply_subtract_fusion.2), channel_id=1, source_target_pairs={{0,8},{8,16},{16,24},{24,0},{1,9},{9,17},{17,25},{25,1},{2,10},{10... | collective-permute-start | bytes 3145736 | tf_op jit(solution)/shard_map/ppermute | solution.py:20
  152.1 20.4 %copy-start.7 = (f32[4,16,32,128]{3,2,1,0:T(8,128)}, f32[4,16,32,128]{3,2,1,0:T(8,128)S(1)}, u32[]{:S(2)}) copy-start(f32[4,16,32,128]{3,2,1,0:T(8,128)S(1)} %collective-permute-done.4) | copy-start | bytes 3145732
  182.7 26.0 %collective-permute-start.6 = (f32[4,16,32,128]{3,2,1,0:T(8,128)S(1)}, f32[4,16,32,128]{3,2,1,0:T(8,128)S(1)}, u32[]{:S(2)}, u32[]{:S(2)}) collective-permute-start(f32[4,16,32,128]{3,2,1,0:T(8,128)S(1)} %multiply_subtract_fusion.1), channel_id=1, source_target_pairs={{8,0},{16,8},{24,16},{0,24},{9,1},{17,9},{25,17},{1,25},{10,2},{18... | collective-permute-start | bytes 3145736 | tf_op jit(solution)/shard_map/ppermute | solution.py:21
  184.1 44.0 %collective-permute-start.7 = (f32[4,16,32,128]{3,2,1,0:T(8,128)S(1)}, f32[4,16,32,128]{3,2,1,0:T(8,128)S(1)}, u32[]{:S(2)}, u32[]{:S(2)}) collective-permute-start(f32[4,16,32,128]{3,2,1,0:T(8,128)S(1)} %multiply_subtract_fusion.1), channel_id=1, source_target_pairs={{0,8},{8,16},{16,24},{24,0},{1,9},{9,17},{17,25},{25,1},{2,10},{10... | collective-permute-start | bytes 3145736 | tf_op jit(solution)/shard_map/ppermute | solution.py:20
  190.3 38.9 %copy-start.13 = (f32[4,16,32]{2,1,0:T(8,128)S(1)}, f32[4,16,32]{2,1,0:T(8,128)}, u32[]{:S(2)}) copy-start(f32[4,16,32]{2,1,0:T(8,128)} %param.3) | copy-start | bytes 24580
  208.7 19.4 %copy-start.6 = (f32[4,16,32,128]{3,2,1,0:T(8,128)}, f32[4,16,32,128]{3,2,1,0:T(8,128)S(1)}, u32[]{:S(2)}) copy-start(f32[4,16,32,128]{3,2,1,0:T(8,128)S(1)} %collective-permute-done.6) | copy-start | bytes 3145732
  237.6 6.8 %collective-permute-start.8 = (f32[2048,64]{0,1:T(8,128)S(1)}, f32[2048,64]{0,1:T(8,128)}, u32[]{:S(2)}, u32[]{:S(2)}) collective-permute-start(f32[2048,64]{0,1:T(8,128)S(1)} %copy.11), channel_id=1, source_target_pairs={{0,7},{1,0},{2,1},{3,2},{4,3},{5,4},{6,5},{7,6},{8,15},{9,8},{10,9... | collective-permute-start | bytes 1572872 | tf_op jit(solution)/shard_map/ppermute | solution.py:65
  246.0 26.2 %collective-permute-start.9 = (f32[2048,128]{1,0:T(8,128)S(1)}, f32[2048,128]{1,0:T(8,128)S(1)}, u32[]{:S(2)}, u32[]{:S(2)}) collective-permute-start(f32[2048,128]{1,0:T(8,128)S(1)} %pad_maximum_fusion.7), channel_id=1, source_target_pairs={{0,6},{1,7},{2,0},{3,1},{4,2},{5,3},{6,4},{7,5},{8,14},{9,15},{10,... | collective-permute-start | bytes 3145736 | tf_op jit(solution)/shard_map/ppermute | solution.py:65
  272.2 2.0 copy-start.1
  274.1 94.2 %collective-permute-start.10 = (f32[2048,256]{1,0:T(8,128)}, f32[2048,256]{1,0:T(8,128)}, u32[]{:S(2)}, u32[]{:S(2)}) collective-permute-start(f32[2048,256]{1,0:T(8,128)} %pad_maximum_fusion), channel_id=1, source_target_pairs={{0,4},{1,5},{2,6},{3,7},{4,0},{5,1},{6,2},{7,3},{8,12},{9,13},{10,... | collective-permute-start | bytes 6291464 | tf_op jit(solution)/shard_map/ppermute | solution.py:65
  453.0 1.8 copy-start.2
  512.1 81.5 %copy-start.4 = (f32[512,512]{1,0:T(8,128)S(1)}, f32[512,512]{1,0:T(8,128)}, u32[]{:S(2)}) copy-start(f32[512,512]{1,0:T(8,128)} %fusion.136) | copy-start | bytes 3145732
  594.0 11.2 %slice-start = ((s8[8388608]{0:T(1024)(128)(4,1)}), s8[4194304]{0:T(1024)(128)(4,1)S(1)}, s32[]{:S(2)}) async-start(s8[8388608]{0:T(1024)(128)(4,1)} %bitcast.52), calls=%async_computation.1 | async-start | bytes 8388608
  596.5 8.8 %slice-start.1 = ((s8[8388608]{0:T(1024)(128)(4,1)}), s8[4194304]{0:T(1024)(128)(4,1)S(1)}, s32[]{:S(2)}) async-start(s8[8388608]{0:T(1024)(128)(4,1)} %bitcast.52), calls=%async_computation.2 | async-start | bytes 8388608
  598.4 6.8 %copy-start.5 = (f32[2048,64]{0,1:T(8,128)S(1)}, f32[2048,64]{0,1:T(8,128)}, u32[]{:S(2)}) copy-start(f32[2048,64]{0,1:T(8,128)} %copy.21) | copy-start | bytes 1572868
  (5 other events, 5.4 us)
Sparse Core Ops, SparseCore 0:
  398.3 54.6 all-reduce.3
